TPU v7x, 256 devices: a whole 4x4x8 slice. The times are simulated.
256 devices in a mesh: dp: 4 (over y), ctx: 32 (over x_hi, z, core), head: 2 (over x_lo).
Axes of the slice: x: 4 (x_hi: 2, x_lo: 2; x = x_hi * 2 + x_lo), y: 4, z: 8, core: 2. Of those that a mesh axis runs over, the one named last changes fastest.
Arguments:
- queries: bfloat16 [4, 8192, 2048], P('dp', 'ctx', 'head'), may hold values from -35 to 35
- key_rows: bfloat16 [4, 8192, 2048], P('dp', 'ctx', 'head'), may hold values from -6 to 6
- value_rows: bfloat16 [4, 8192, 2048], P('dp', 'ctx', 'head'), may hold values from -6 to 6
- sink_logits: float32 [16], P('head'), may hold values from 4 to 9
- partner: int32 [3, 32], replicated, may hold values from 0 to 31, as said below
- block_pick: int32 [4, 3, 32], P('dp'), may hold values from 0 to 1
- out_grad: bfloat16 [4, 8192, 2048], P('dp', 'ctx', 'head'), may hold values from -18 to 18
Outputs:
- attention: bfloat16 [4, 8192, 2048], P('dp', 'ctx', 'head')
- query_grad: bfloat16 [4, 8192, 2048], P('dp', 'ctx', 'head')
- key_grad: bfloat16 [4, 8192, 2048], P('dp', 'ctx', 'head')
- value_grad: bfloat16 [4, 8192, 2048], P('dp', 'ctx', 'head')
- sink_grad: float32 [16], P('head')
Inputs may be any that keep to these rules, and one draw needn't show every extreme that they name: partner[r, i] = i XOR partner[r, 0] for every round r, and partner[r, 0] is a power of two: each round pairs the indices of ctx that differ in one bit.
All inputs are finite; a program needn't handle non-finite values.
Results may differ from a plain program's by a relative error of at most 0.0093.
Values may be sent and summed in bfloat16 or wider, within the bound.
No kernel may reach another device: no remote copies, remote signals or barrier semaphores. Data moves between devices by JAX's collectives and lax.ppermute only.
A program may use at most 128 MiB of HBM per device.

v0:
```python
import math
import jax
import jax.numpy as jnp
from jax import lax
from jax.sharding import PartitionSpec as P

HD = 128
BLOCK = 128
ROUNDS = 3


def partner_2(value, axis, apart):
    mask = 2**apart
    pairs = [(source, source ^ mask) for source in range(lax.axis_size(axis))]
    return lax.ppermute(value, axis, pairs)


def broadcast(value, axis, source):
    kept = jnp.where(lax.axis_index(axis) == source, value, 0).astype(value.dtype)
    return lax.psum(kept, axis)


def padded(shard, sides, width):
    for axis, dim in sides:
        peers, length = (lax.axis_size(axis), shard.shape[dim])
        up = [(i, (i + 1) % peers) for i in range(peers - 1)]
        down = [(j, i) for i, j in up]
        last = lax.slice_in_dim(shard, length - width, length, axis=dim)
        leading = lax.slice_in_dim(shard, 0, width, axis=dim)
        before = lax.ppermute(last, axis, up)
        after = lax.ppermute(leading, axis, down)
        shard = jnp.concatenate([before, shard, after], axis=dim)
    return shard


def passed_along(shard, axis, by):
    peers = lax.axis_size(axis)
    pairs = [(i, i + by) for i in range(peers) if 0 <= i + by < peers]
    return lax.ppermute(shard, axis, pairs)


def to_heads(matrix, head_count):
    return matrix.reshape(matrix.shape[0], head_count, HD).transpose(1, 0, 2)


def from_heads(tensor):
    return tensor.transpose(1, 0, 2).reshape(tensor.shape[1], tensor.shape[0] * tensor.shape[2])


def place_rows(piece, start, length_total):
    widths = [(0, 0)] * piece.ndim
    widths[piece.ndim - 2] = (start, length_total - start - piece.shape[-2])
    return jnp.pad(piece, widths)


def route_apart(package, xor_mask, bit_count):
    for bit_place in range(bit_count):
        arrived = partner_2(package, "ctx", bit_place)
        package = jnp.where(jnp.right_shift(xor_mask, bit_place) % 2 == 1, arrived, package)
    return package


def return_apart(package, xor_mask, bit_count):
    for bit_place in range(bit_count):
        arrived = partner_2(package, "ctx", bit_place)
        package = jnp.where(jnp.right_shift(xor_mask, bit_place) % 2 == 1, arrived, package)
    return package


def body(queries, key_rows, value_rows, sink_logits, partner, block_pick, out_grad):
    own_query = queries[0]
    own_keys = key_rows[0]
    own_values = value_rows[0]
    own_grad = out_grad[0]
    tokens = own_query.shape[0]
    feature_width = own_query.shape[1]
    head_count = feature_width // HD
    shard_blocks = tokens // BLOCK
    ctx_count = lax.axis_size("ctx")
    ctx_place = lax.axis_index("ctx")
    bit_count = ctx_count.bit_length() - 1
    scaling = HD ** (-0.5)
    is_first = ctx_place == 0
    is_last = ctx_place == ctx_count - 1
    slot_count = (5 + ROUNDS) * BLOCK
    first_pack = jnp.stack(
        [own_query[:BLOCK], own_keys[:BLOCK], own_values[:BLOCK], own_grad[:BLOCK]]
    )
    last_pack = jnp.stack(
        [
            own_query[tokens - BLOCK :],
            own_keys[tokens - BLOCK :],
            own_values[tokens - BLOCK :],
            own_grad[tokens - BLOCK :],
        ]
    )
    first_got = broadcast(first_pack, "ctx", 0)
    last_got = broadcast(last_pack, "ctx", ctx_count - 1)
    global_pack = jnp.concatenate([first_got, last_got], axis=1)
    global_query = to_heads(global_pack[0], head_count)
    global_grad = to_heads(global_pack[3], head_count)
    pair_rows = jnp.concatenate([own_keys, own_values], axis=1)
    extended = padded(pair_rows, (("ctx", 0),), BLOCK)
    xor_masks = partner[:, 0]
    partner_place = jnp.bitwise_xor(ctx_place, xor_masks)
    ctx_match = jnp.arange(ctx_count)[None, :] == partner_place[:, None]
    wanted = jnp.sum(jnp.where(ctx_match, block_pick[0], 0), axis=1)
    packages = jnp.stack(
        [
            lax.dynamic_slice_in_dim(pair_rows, wanted[number] * BLOCK, BLOCK, 0)
            for number in range(ROUNDS)
        ]
    )
    fetched = jnp.stack(
        [route_apart(packages[number], xor_masks[number], bit_count) for number in range(ROUNDS)]
    )
    global_pair = jnp.concatenate([global_pack[1], global_pack[2]], axis=1)
    shared_pair = jnp.concatenate(
        [global_pair, fetched.reshape(ROUNDS * BLOCK, 2 * feature_width)], axis=0
    )
    window_pair = jnp.stack(
        [
            extended[step * BLOCK : step * BLOCK + tokens].reshape(
                shard_blocks, BLOCK, 2 * feature_width
            )
            for step in range(3)
        ],
        axis=1,
    ).reshape(shard_blocks, 3 * BLOCK, 2 * feature_width)
    slot_pair = jnp.concatenate(
        [
            window_pair,
            jnp.broadcast_to(
                shared_pair[None], (shard_blocks, (2 + ROUNDS) * BLOCK, 2 * feature_width)
            ),
        ],
        axis=1,
    )
    slot_keys = (
        slot_pair[:, :, :feature_width]
        .reshape(shard_blocks, slot_count, head_count, HD)
        .transpose(2, 0, 1, 3)
    )
    slot_values = (
        slot_pair[:, :, feature_width:]
        .reshape(shard_blocks, slot_count, head_count, HD)
        .transpose(2, 0, 1, 3)
    )
    query_heads = to_heads(own_query, head_count)
    query_blocks = query_heads.reshape(head_count, shard_blocks, BLOCK, HD)
    key_heads = to_heads(own_keys, head_count)
    value_heads = to_heads(own_values, head_count)
    block_index = jnp.arange(shard_blocks)
    prev_ok = jnp.logical_not(is_first & (block_index == 1))
    next_ok = jnp.logical_not(is_last & (block_index == shard_blocks - 2))
    slot_valid = jnp.concatenate(
        [
            jnp.broadcast_to(prev_ok[:, None], (shard_blocks, BLOCK)),
            jnp.ones((shard_blocks, BLOCK), bool),
            jnp.broadcast_to(next_ok[:, None], (shard_blocks, BLOCK)),
            jnp.ones((shard_blocks, (2 + ROUNDS) * BLOCK), bool),
        ],
        axis=1,
    )
    sink_grid = sink_logits[:, None, None]
    scores = (
        jnp.einsum("hnqd,hnkd->hnqk", query_blocks, slot_keys, preferred_element_type=jnp.float32)
        * scaling
    )
    scores = jnp.where(slot_valid[None, :, None, :], scores, -jnp.inf)
    row_top = jnp.maximum(sink_grid, jnp.max(scores, axis=3))
    expo = jnp.exp(scores - row_top[..., None])
    row_total = jnp.exp(sink_grid - row_top) + jnp.sum(expo, axis=3)
    regular_acc = jnp.einsum(
        "hnqk,hnkd->hnqd",
        expo.astype(jnp.bfloat16),
        slot_values,
        preferred_element_type=jnp.float32,
    )
    regular_out = (regular_acc / row_total[..., None]).reshape(head_count, tokens, HD)
    regular_lse = (row_top + jnp.log(row_total)).reshape(head_count, tokens)
    global_scores = (
        jnp.einsum("hgd,htd->hgt", global_query, key_heads, preferred_element_type=jnp.float32)
        * scaling
    )
    local_top = jnp.max(global_scores, axis=2)
    global_top = jnp.maximum(lax.pmax(local_top, "ctx"), sink_logits[:, None])
    global_expo = jnp.exp(global_scores - global_top[..., None])
    part_total = jnp.sum(global_expo, axis=2)
    part_acc = jnp.einsum(
        "hgt,htd->hgd",
        global_expo.astype(jnp.bfloat16),
        value_heads,
        preferred_element_type=jnp.float32,
    )
    summed_total, summed_acc = lax.psum((part_total, part_acc), "ctx")
    global_total = jnp.exp(sink_logits[:, None] - global_top) + summed_total
    global_out = summed_acc / global_total[..., None]
    global_lse = global_top + jnp.log(global_total)
    row_index = jnp.arange(tokens)
    first_rows = is_first & (row_index < BLOCK)
    last_rows = is_last & (row_index >= tokens - BLOCK)
    regular_rows = jnp.logical_not(first_rows | last_rows)
    out_heads = jnp.where(
        first_rows[None, :, None],
        place_rows(global_out[:, :BLOCK], 0, tokens),
        jnp.where(
            last_rows[None, :, None],
            place_rows(global_out[:, BLOCK:], tokens - BLOCK, tokens),
            regular_out,
        ),
    )
    attention_half = out_heads.astype(jnp.bfloat16)
    lse_rows = jnp.where(
        first_rows[None, :],
        jnp.pad(global_lse[:, :BLOCK], ((0, 0), (0, tokens - BLOCK))),
        jnp.where(
            last_rows[None, :],
            jnp.pad(global_lse[:, BLOCK:], ((0, 0), (tokens - BLOCK, 0))),
            regular_lse,
        ),
    )
    grad_heads = to_heads(own_grad, head_count)
    row_delta = jnp.sum(grad_heads.astype(jnp.float32) * attention_half.astype(jnp.float32), axis=2)
    grad_regular = jnp.where(regular_rows[None, :, None], grad_heads, jnp.zeros_like(grad_heads))
    grad_blocks = grad_regular.reshape(head_count, shard_blocks, BLOCK, HD)
    delta_blocks = jnp.where(regular_rows[None, :], row_delta, 0.0).reshape(
        head_count, shard_blocks, BLOCK
    )
    lse_blocks = regular_lse.reshape(head_count, shard_blocks, BLOCK)
    probs = jnp.exp(scores - lse_blocks[..., None])
    prob_grad = jnp.einsum(
        "hnqd,hnkd->hnqk", grad_blocks, slot_values, preferred_element_type=jnp.float32
    )
    score_grad = (probs * (prob_grad - delta_blocks[..., None])).astype(jnp.bfloat16)
    prob_half = probs.astype(jnp.bfloat16)
    regular_dq = (
        jnp.einsum("hnqk,hnkd->hnqd", score_grad, slot_keys, preferred_element_type=jnp.float32)
        * scaling
    ).reshape(head_count, tokens, HD)
    slot_dk = (
        jnp.einsum("hnqk,hnqd->hnkd", score_grad, query_blocks, preferred_element_type=jnp.float32)
        * scaling
    )
    slot_dv = jnp.einsum(
        "hnqk,hnqd->hnkd", prob_half, grad_blocks, preferred_element_type=jnp.float32
    )
    slot_both = jnp.stack([slot_dk, slot_dv])
    window_lower = slot_both[:, :, :, :BLOCK].reshape(2, head_count, tokens, HD)
    window_self = slot_both[:, :, :, BLOCK : 2 * BLOCK].reshape(2, head_count, tokens, HD)
    window_upper = slot_both[:, :, :, 2 * BLOCK : 3 * BLOCK].reshape(2, head_count, tokens, HD)
    from_above = passed_along(window_lower[:, :, :BLOCK].astype(jnp.bfloat16), "ctx", -1).astype(
        jnp.float32
    )
    from_below = passed_along(window_upper[:, :, tokens - BLOCK :], "ctx", 1)
    key_pair = (
        window_self
        + jnp.concatenate([window_lower[:, :, BLOCK:], from_above], axis=2)
        + jnp.concatenate([from_below, window_upper[:, :, : tokens - BLOCK]], axis=2)
    )
    global_slots = jnp.sum(slot_both[:, :, :, 3 * BLOCK : 5 * BLOCK], axis=2)
    random_pack = (
        jnp.sum(
            slot_both[:, :, :, 5 * BLOCK :].reshape(2, head_count, shard_blocks, ROUNDS, BLOCK, HD),
            axis=2,
        )
        .transpose(2, 0, 1, 3, 4)
        .astype(jnp.bfloat16)
    )
    global_probs = jnp.exp(global_scores - global_lse[..., None])
    global_att = global_out.astype(jnp.bfloat16)
    global_delta = jnp.sum(global_grad.astype(jnp.float32) * global_att.astype(jnp.float32), axis=2)
    global_dp = jnp.einsum(
        "hgd,htd->hgt", global_grad, value_heads, preferred_element_type=jnp.float32
    )
    global_ds = (global_probs * (global_dp - global_delta[..., None])).astype(jnp.bfloat16)
    part_dq = (
        jnp.einsum("hgt,htd->hgd", global_ds, key_heads, preferred_element_type=jnp.float32)
        * scaling
    )
    owned_dk = (
        jnp.einsum("hgt,hgd->htd", global_ds, global_query, preferred_element_type=jnp.float32)
        * scaling
    )
    owned_dv = jnp.einsum(
        "hgt,hgd->htd",
        global_probs.astype(jnp.bfloat16),
        global_grad,
        preferred_element_type=jnp.float32,
    )
    key_pair = key_pair + jnp.stack([owned_dk, owned_dv])
    summed_dq, summed_slots = lax.psum((part_dq, global_slots), "ctx")
    key_pair = key_pair + is_first.astype(jnp.float32) * place_rows(
        summed_slots[:, :, :BLOCK], 0, tokens
    )
    key_pair = key_pair + is_last.astype(jnp.float32) * place_rows(
        summed_slots[:, :, BLOCK:], tokens - BLOCK, tokens
    )
    returned = jnp.stack(
        [
            return_apart(random_pack[number], xor_masks[number], bit_count)
            for number in range(ROUNDS)
        ]
    )
    block_match = (jnp.arange(shard_blocks)[None, :] == wanted[:, None]).astype(jnp.float32)
    random_add = jnp.einsum("rn,rchbd->chnbd", block_match, returned.astype(jnp.float32)).reshape(
        2, head_count, tokens, HD
    )
    key_pair = key_pair + random_add
    query_total = jnp.where(
        first_rows[None, :, None],
        place_rows(summed_dq[:, :BLOCK], 0, tokens),
        jnp.where(
            last_rows[None, :, None],
            place_rows(summed_dq[:, BLOCK:], tokens - BLOCK, tokens),
            regular_dq,
        ),
    )
    sink_part = -jnp.sum(jnp.exp(sink_logits[:, None] - lse_rows) * row_delta, axis=1)
    sink_total = lax.psum(sink_part, ("dp", "ctx"))
    sink_grad = sink_total / math.sqrt(lax.axis_size("dp") * ctx_count * tokens)
    attention = from_heads(attention_half)[None]
    query_grad = from_heads(query_total.astype(jnp.bfloat16))[None]
    key_grad = from_heads(key_pair[0].astype(jnp.bfloat16))[None]
    value_grad = from_heads(key_pair[1].astype(jnp.bfloat16))[None]
    return (attention, query_grad, key_grad, value_grad, sink_grad)


def solution(mesh):
    return jax.shard_map(
        body,
        mesh=mesh,
        in_specs=(
            P("dp", "ctx", "head"),
            P("dp", "ctx", "head"),
            P("dp", "ctx", "head"),
            P("head"),
            P(),
            P("dp", None, None),
            P("dp", "ctx", "head"),
        ),
        out_specs=(
            P("dp", "ctx", "head"),
            P("dp", "ctx", "head"),
            P("dp", "ctx", "head"),
            P("dp", "ctx", "head"),
            P("head"),
        ),
        check_vma=False,
    )
```

profile of v0, /device:TPU:1, one launch (start us, length us, event | category | flops | bytes accessed | tf_op | source)
XLA Modules:
  0.0 1673.2 jit_solution(2412980870164297198)
XLA Ops:
  66.8 18.6 %collective-permute-done.8 = bf16[128,2048]{1,0:T(8,128)(2,1)} collective-permute-done((bf16[128,2048]{1,0:T(8,128)(2,1)}, bf16[128,2048]{1,0:T(8,128)(2,1)}, u32[]{:S(2)}, u32[]{:S(2)}) %collective-permute-start.8) | collective-permute-done | bytes 524320 | tf_op jit(solution)/shard_map/ppermute | solution.py:15
  90.6 8.0 collective-permute-done.13
  108.9 51.2 %collective-permute-done.9 = bf16[128,2048]{1,0:T(8,128)(2,1)S(1)} collective-permute-done((bf16[128,2048]{1,0:T(8,128)(2,1)S(1)}, bf16[128,2048]{1,0:T(8,128)(2,1)S(1)}, u32[]{:S(2)}, u32[]{:S(2)}) %collective-permute-start.9) | collective-permute-done | bytes 524320 | tf_op jit(solution)/shard_map/ppermute | solution.py:15
  164.5 21.6 %collective-permute-done.14 = bf16[128,2048]{1,0:T(8,128)(2,1)S(1)} collective-permute-done((bf16[128,2048]{1,0:T(8,128)(2,1)S(1)}, bf16[128,2048]{1,0:T(8,128)(2,1)S(1)}, u32[]{:S(2)}, u32[]{:S(2)}) %collective-permute-start.14) | collective-permute-done | bytes 524320 | tf_op jit(solution)/shard_map/ppermute | solution.py:15
  190.6 183.5 %all-reduce.14.cloned.1.call-done = (bf16[4,128,1024]{1,2,0:T(8,128)(2,1)}, bf16[4,128,1024]{1,2,0:T(8,128)(2,1)}) async-done(((bf16[4,128,1024]{1,2,0:T(8,128)(2,1)}, bf16[4,128,1024]{1,2,0:T(8,128)(2,1)}), (bf16[4,128,1024]{1,2,0:T(8,128)(2,1)}, bf16[4,128,1024]{1,2,0:T(8,128)(2,1)})) %all-reduce.14.cloned.1.call-update) | async-done | bytes 2097168 | tf_op jit(solution)/shard_map/psum | solution.py:20
  380.7 66.2 %pmax.7 = f32[8,256]{1,0:T(8,128)S(1)} all-reduce(f32[8,256]{1,0:T(8,128)S(1)} %get-tuple-element.72), channel_id=1, replica_groups=mesh['dp'=4,'ctx'=32,'head'=2] {'ctx'}, use_global_device_ids=true, to_apply=%region_3.4 | all-reduce | flops 2048 | bytes 16384 | tf_op jit(solution)/shard_map/pmax | solution.py:187
  447.3 71.4 %psum.52 = f32[8,256]{1,0:T(8,128)S(1)} all-reduce(f32[8,256]{1,0:T(8,128)S(1)} %fusion.38), channel_id=1, replica_groups=mesh['dp'=4,'ctx'=32,'head'=2] {'ctx'}, use_global_device_ids=true, to_apply=%region_6.7 | all-reduce | flops 2048 | bytes 16384 | tf_op jit(solution)/shard_map/psum | solution.py:196
  529.0 9.0 collective-permute-done.6
  538.1 11.5 collective-permute-done.11
  549.7 11.9 collective-permute-done.16
  573.4 6.5 copy.137
  590.8 6.5 copy.139
  597.2 8.3 fusion.56
  605.6 182.0 %all-reduce.10.cloned.1.call-done = f32[8,256,128]{2,1,0:T(8,128)} async-done(((f32[8,256,128]{2,1,0:T(8,128)}), f32[8,256,128]{2,1,0:T(8,128)}) %all-reduce.10.cloned.1.call-update) | async-done | bytes 1048592 | tf_op jit(solution)/shard_map/psum | solution.py:196
  811.4 139.2 %all-reduce.15 = bf16[8,256,128]{2,1,0:T(8,128)(2,1)S(1)} all-reduce(f32[8,256,128]{2,1,0:T(8,128)} %convolution_multiply_fusion.2), channel_id=1, replica_groups=mesh['dp'=4,'ctx'=32,'head'=2] {'ctx'}, use_global_device_ids=true, to_apply=%region_11.12 | all-reduce | flops 262144 | bytes 1572864 | tf_op jit(solution)/shard_map/psum | solution.py:292
  951.1 6.2 collective-permute-start.19
  973.2 328.8 %psum.55 = f32[8]{0:T(128)S(1)} all-reduce(f32[8]{0:T(128)S(1)} %neg.3), channel_id=1, replica_groups=mesh['dp'=4,'ctx'=32,'head'=2] {'dp','ctx'}, use_global_device_ids=true, to_apply=%region_17.18 | all-reduce | flops 8 | bytes 64 | tf_op jit(solution)/shard_map/psum | solution.py:320
  1315.1 22.8 %collective-permute-done.25 = bf16[2,8,128,128]{3,2,1,0:T(8,128)(2,1)S(1)} collective-permute-done((bf16[2,8,128,128]{3,2,1,0:T(8,128)(2,1)}, bf16[2,8,128,128]{3,2,1,0:T(8,128)(2,1)S(1)}, u32[]{:S(2)}, u32[]{:S(2)}) %collective-permute-start.25) | collective-permute-done | bytes 524320 | tf_op jit(solution)/shard_map/ppermute | solution.py:15
  1339.8 78.2 %collective-permute-done.21 = bf16[2,8,128,128]{3,2,1,0:T(8,128)(2,1)S(1)} collective-permute-done((bf16[2,8,128,128]{3,2,1,0:T(8,128)(2,1)S(1)}, bf16[2,8,128,128]{3,2,1,0:T(8,128)(2,1)S(1)}, u32[]{:S(2)}, u32[]{:S(2)}) %collective-permute-start.21) | collective-permute-done | bytes 524320 | tf_op jit(solution)/shard_map/ppermute | solution.py:15
  1418.2 23.5 %collective-permute-done.31 = bf16[2,8,128,128]{3,2,1,0:T(8,128)(2,1)S(1)} collective-permute-done((bf16[2,8,128,128]{3,2,1,0:T(8,128)(2,1)S(1)}, bf16[2,8,128,128]{3,2,1,0:T(8,128)(2,1)S(1)}, u32[]{:S(2)}, u32[]{:S(2)}) %collective-permute-start.31) | collective-permute-done | bytes 524320 | tf_op jit(solution)/shard_map/ppermute | solution.py:15
  1441.8 12.2 collective-permute-done.26
  1454.4 26.7 %collective-permute-done.32 = bf16[2,8,128,128]{3,2,1,0:T(8,128)(2,1)S(1)} collective-permute-done((bf16[2,8,128,128]{3,2,1,0:T(8,128)(2,1)S(1)}, bf16[2,8,128,128]{3,2,1,0:T(8,128)(2,1)S(1)}, u32[]{:S(2)}, u32[]{:S(2)}) %collective-permute-start.32) | collective-permute-done | bytes 524320 | tf_op jit(solution)/shard_map/ppermute | solution.py:15
  1482.0 15.6 collective-permute-done.27
  1498.5 152.1 %all-reduce.12.cloned.1.call-done = f32[2,8,256,128]{3,2,1,0:T(8,128)} async-done(((f32[2,8,256,128]{3,2,1,0:T(8,128)}), f32[2,8,256,128]{3,2,1,0:T(8,128)}) %all-reduce.12.cloned.1.call-update) | async-done | bytes 2097168 | tf_op jit(solution)/shard_map/psum | solution.py:292
  (267 shorter events, 185.1 us)
Async XLA Ops:
  7.2 366.9 %all-reduce.14.cloned.1.call-start = ((), (), s32[]{:S(2)}) async-start(), calls=%async_computation.2 | async-start | bytes 4194304 | tf_op jit(solution)/shard_map/psum | solution.py:20
  15.1 38.1 %collective-permute-start = (bf16[128,2048]{1,0:T(8,128)(2,1)}, bf16[128,2048]{1,0:T(8,128)(2,1)}, u32[]{:S(2)}, u32[]{:S(2)}) collective-permute-start(bf16[128,2048]{1,0:T(8,128)(2,1)} %get-tuple-element.51), channel_id=1, source_target_pairs={{0,2},{2,4},{4,6},{6,8},{8,10},{10,12},{12,14},{14,16},{16,18},{18... | collective-permute-start | bytes 1572872 | tf_op jit(solution)/shard_map/ppermute | solution.py:30
  30.4 757.2 %all-reduce.10.cloned.1.call-start = ((), (), s32[]{:S(2)}) async-start(), calls=%async_computation | async-start | bytes 2097152 | tf_op jit(solution)/shard_map/psum | solution.py:196
  51.7 47.0 %collective-permute-start.13 = (bf16[128,2048]{1,0:T(8,128)(2,1)}, bf16[128,2048]{1,0:T(8,128)(2,1)}, u32[]{:S(2)}, u32[]{:S(2)}) collective-permute-start(bf16[128,2048]{1,0:T(8,128)(2,1)} %broadcast_select_fusion.12), channel_id=1, source_target_pairs={{0,4},{2,6},{4,0},{6,2},{8,12},{10,14},{12,8},{14,10},{16,20},{18,... | collective-permute-start | bytes 1572872 | tf_op jit(solution)/shard_map/ppermute | solution.py:15
  62.6 40.4 %collective-permute-start.4 = (bf16[128,2048]{1,0:T(8,128)(2,1)S(1)}, bf16[128,2048]{1,0:T(8,128)(2,1)S(1)}, u32[]{:S(2)}, u32[]{:S(2)}) collective-permute-start(bf16[128,2048]{1,0:T(8,128)(2,1)S(1)} %broadcast_select_fusion.21), channel_id=1, source_target_pairs={{0,8},{2,10},{4,12},{6,14},{8,0},{10,2},{12,4},{14,6},{16,24},{18,... | collective-permute-start | bytes 1572872 | tf_op jit(solution)/shard_map/ppermute | solution.py:15
  86.5 73.6 %collective-permute-start.9 = (bf16[128,2048]{1,0:T(8,128)(2,1)S(1)}, bf16[128,2048]{1,0:T(8,128)(2,1)S(1)}, u32[]{:S(2)}, u32[]{:S(2)}) collective-permute-start(bf16[128,2048]{1,0:T(8,128)(2,1)S(1)} %broadcast_select_fusion.17), channel_id=1, source_target_pairs={{0,8},{2,10},{4,12},{6,14},{8,0},{10,2},{12,4},{14,6},{16,24},{18,... | collective-permute-start | bytes 1572872 | tf_op jit(solution)/shard_map/ppermute | solution.py:15
  99.7 86.3 %collective-permute-start.14 = (bf16[128,2048]{1,0:T(8,128)(2,1)S(1)}, bf16[128,2048]{1,0:T(8,128)(2,1)S(1)}, u32[]{:S(2)}, u32[]{:S(2)}) collective-permute-start(bf16[128,2048]{1,0:T(8,128)(2,1)S(1)} %broadcast_select_fusion.13), channel_id=1, source_target_pairs={{0,8},{2,10},{4,12},{6,14},{8,0},{10,2},{12,4},{14,6},{16,24},{18,... | collective-permute-start | bytes 1572872 | tf_op jit(solution)/shard_map/ppermute | solution.py:15
  103.8 418.3 %collective-permute-start.5 = (bf16[128,2048]{1,0:T(8,128)(2,1)}, bf16[128,2048]{1,0:T(8,128)(2,1)}, u32[]{:S(2)}, u32[]{:S(2)}) collective-permute-start(bf16[128,2048]{1,0:T(8,128)(2,1)} %broadcast_select_fusion.22), channel_id=1, source_target_pairs={{0,16},{2,18},{4,20},{6,22},{8,24},{10,26},{12,28},{14,30},{16,0},... | collective-permute-start | bytes 1572872 | tf_op jit(solution)/shard_map/ppermute | solution.py:15
  161.0 362.7 %collective-permute-start.10 = (bf16[128,2048]{1,0:T(8,128)(2,1)}, bf16[128,2048]{1,0:T(8,128)(2,1)}, u32[]{:S(2)}, u32[]{:S(2)}) collective-permute-start(bf16[128,2048]{1,0:T(8,128)(2,1)} %broadcast_select_fusion.18), channel_id=1, source_target_pairs={{0,16},{2,18},{4,20},{6,22},{8,24},{10,26},{12,28},{14,30},{16,0},... | collective-permute-start | bytes 1572872 | tf_op jit(solution)/shard_map/ppermute | solution.py:15
  186.9 340.6 %collective-permute-start.15 = (bf16[128,2048]{1,0:T(8,128)(2,1)}, bf16[128,2048]{1,0:T(8,128)(2,1)}, u32[]{:S(2)}, u32[]{:S(2)}) collective-permute-start(bf16[128,2048]{1,0:T(8,128)(2,1)} %broadcast_select_fusion.14), channel_id=1, source_target_pairs={{0,16},{2,18},{4,20},{6,22},{8,24},{10,26},{12,28},{14,30},{16,0},... | collective-permute-start | bytes 1572872 | tf_op jit(solution)/shard_map/ppermute | solution.py:15
  522.0 1128.5 %all-reduce.12.cloned.1.call-start = ((), (), s32[]{:S(2)}) async-start(), calls=%async_computation.1 | async-start | bytes 4194304 | tf_op jit(solution)/shard_map/psum | solution.py:292
  959.9 349.2 %collective-permute-start.17 = (bf16[2,8,128,128]{3,2,1,0:T(8,128)(2,1)}, bf16[2,8,128,128]{3,2,1,0:T(8,128)(2,1)}, u32[]{:S(2)}, u32[]{:S(2)}) collective-permute-start(bf16[2,8,128,128]{3,2,1,0:T(8,128)(2,1)} %slice.260), channel_id=1, source_target_pairs={{2,0},{4,2},{6,4},{8,6},{10,8},{12,10},{14,12},{16,14},{18,16},{20... | collective-permute-start | bytes 1572872 | tf_op jit(solution)/shard_map/ppermute | solution.py:39
  968.6 341.6 %collective-permute-start.20 = (bf16[2,8,128,128]{3,2,1,0:T(8,128)(2,1)}, bf16[2,8,128,128]{3,2,1,0:T(8,128)(2,1)}, u32[]{:S(2)}, u32[]{:S(2)}) collective-permute-start(bf16[2,8,128,128]{3,2,1,0:T(8,128)(2,1)} %get-tuple-element.41), channel_id=1, source_target_pairs={{0,4},{2,6},{4,0},{6,2},{8,12},{10,14},{12,8},{14,10},{16,20},{18,... | collective-permute-start | bytes 1572872 | tf_op jit(solution)/shard_map/ppermute | solution.py:15
  970.1 341.5 %collective-permute-start.30 = (bf16[2,8,128,128]{3,2,1,0:T(8,128)(2,1)}, bf16[2,8,128,128]{3,2,1,0:T(8,128)(2,1)}, u32[]{:S(2)}, u32[]{:S(2)}) collective-permute-start(bf16[2,8,128,128]{3,2,1,0:T(8,128)(2,1)} %get-tuple-element.42), channel_id=1, source_target_pairs={{0,4},{2,6},{4,0},{6,2},{8,12},{10,14},{12,8},{14,10},{16,20},{18,... | collective-permute-start | bytes 1572872 | tf_op jit(solution)/shard_map/ppermute | solution.py:15
  1306.6 353.3 %collective-permute-start.18 = (f32[2,8,128,128]{3,2,1,0:T(8,128)}, f32[2,8,128,128]{3,2,1,0:T(8,128)}, u32[]{:S(2)}, u32[]{:S(2)}) collective-permute-start(f32[2,8,128,128]{3,2,1,0:T(8,128)} %get-tuple-element.35), channel_id=1, source_target_pairs={{0,2},{2,4},{4,6},{6,8},{8,10},{10,12},{12,14},{14,16},{16,18},{18... | collective-permute-start | bytes 3145736 | tf_op jit(solution)/shard_map/ppermute | solution.py:39
  1311.3 106.7 %collective-permute-start.21 = (bf16[2,8,128,128]{3,2,1,0:T(8,128)(2,1)S(1)}, bf16[2,8,128,128]{3,2,1,0:T(8,128)(2,1)S(1)}, u32[]{:S(2)}, u32[]{:S(2)}) collective-permute-start(bf16[2,8,128,128]{3,2,1,0:T(8,128)(2,1)S(1)} %broadcast_select_fusion.9), channel_id=1, source_target_pairs={{0,8},{2,10},{4,12},{6,14},{8,0},{10,2},{12,4},{14,6},{16,24},{18,... | collective-permute-start | bytes 1572872 | tf_op jit(solution)/shard_map/ppermute | solution.py:15
  1312.7 129.0 %collective-permute-start.31 = (bf16[2,8,128,128]{3,2,1,0:T(8,128)(2,1)S(1)}, bf16[2,8,128,128]{3,2,1,0:T(8,128)(2,1)S(1)}, u32[]{:S(2)}, u32[]{:S(2)}) collective-permute-start(bf16[2,8,128,128]{3,2,1,0:T(8,128)(2,1)S(1)} %broadcast_select_fusion.1), channel_id=1, source_target_pairs={{0,8},{2,10},{4,12},{6,14},{8,0},{10,2},{12,4},{14,6},{16,24},{18,... | collective-permute-start | bytes 1572872 | tf_op jit(solution)/shard_map/ppermute | solution.py:15
  1339.0 115.0 %collective-permute-start.26 = (bf16[2,8,128,128]{3,2,1,0:T(8,128)(2,1)S(1)}, bf16[2,8,128,128]{3,2,1,0:T(8,128)(2,1)S(1)}, u32[]{:S(2)}, u32[]{:S(2)}) collective-permute-start(bf16[2,8,128,128]{3,2,1,0:T(8,128)(2,1)S(1)} %broadcast_select_fusion.5), channel_id=1, source_target_pairs={{0,8},{2,10},{4,12},{6,14},{8,0},{10,2},{12,4},{14,6},{16,24},{18,... | collective-permute-start | bytes 1572872 | tf_op jit(solution)/shard_map/ppermute | solution.py:15
  1418.1 36.1 %collective-permute-start.22 = (bf16[2,8,128,128]{3,2,1,0:T(8,128)(2,1)S(1)}, bf16[2,8,128,128]{3,2,1,0:T(8,128)(2,1)S(1)}, u32[]{:S(2)}, u32[]{:S(2)}) collective-permute-start(bf16[2,8,128,128]{3,2,1,0:T(8,128)(2,1)S(1)} %broadcast_select_fusion.10), channel_id=1, source_target_pairs={{0,16},{2,18},{4,20},{6,22},{8,24},{10,26},{12,28},{14,30},{16,0},... | collective-permute-start | bytes 1572872 | tf_op jit(solution)/shard_map/ppermute | solution.py:15
  1441.7 39.4 %collective-permute-start.32 = (bf16[2,8,128,128]{3,2,1,0:T(8,128)(2,1)S(1)}, bf16[2,8,128,128]{3,2,1,0:T(8,128)(2,1)S(1)}, u32[]{:S(2)}, u32[]{:S(2)}) collective-permute-start(bf16[2,8,128,128]{3,2,1,0:T(8,128)(2,1)S(1)} %broadcast_select_fusion.2), channel_id=1, source_target_pairs={{0,16},{2,18},{4,20},{6,22},{8,24},{10,26},{12,28},{14,30},{16,0},... | collective-permute-start | bytes 1572872 | tf_op jit(solution)/shard_map/ppermute | solution.py:15
  1454.1 43.5 %collective-permute-start.27 = (bf16[2,8,128,128]{3,2,1,0:T(8,128)(2,1)S(1)}, bf16[2,8,128,128]{3,2,1,0:T(8,128)(2,1)S(1)}, u32[]{:S(2)}, u32[]{:S(2)}) collective-permute-start(bf16[2,8,128,128]{3,2,1,0:T(8,128)(2,1)S(1)} %broadcast_select_fusion.6), channel_id=1, source_target_pairs={{0,16},{2,18},{4,20},{6,22},{8,24},{10,26},{12,28},{14,30},{16,0},... | collective-permute-start | bytes 1572872 | tf_op jit(solution)/shard_map/ppermute | solution.py:15
  1454.3 196.3 %collective-permute-start.23 = (bf16[2,8,128,128]{3,2,1,0:T(8,128)(2,1)S(1)}, bf16[2,8,128,128]{3,2,1,0:T(8,128)(2,1)}, u32[]{:S(2)}, u32[]{:S(2)}) collective-permute-start(bf16[2,8,128,128]{3,2,1,0:T(8,128)(2,1)S(1)} %broadcast_select_fusion.11), channel_id=1, source_target_pairs={{0,32},{2,34},{4,36},{6,38},{8,40},{10,42},{12,44},{14,46},{16,48}... | collective-permute-start | bytes 1572872 | tf_op jit(solution)/shard_map/ppermute | solution.py:15
  1482.0 169.6 %collective-permute-start.33 = (bf16[2,8,128,128]{3,2,1,0:T(8,128)(2,1)}, bf16[2,8,128,128]{3,2,1,0:T(8,128)(2,1)}, u32[]{:S(2)}, u32[]{:S(2)}) collective-permute-start(bf16[2,8,128,128]{3,2,1,0:T(8,128)(2,1)} %broadcast_select_fusion.3), channel_id=1, source_target_pairs={{0,32},{2,34},{4,36},{6,38},{8,40},{10,42},{12,44},{14,46},{16,48}... | collective-permute-start | bytes 1572872 | tf_op jit(solution)/shard_map/ppermute | solution.py:15
  1498.5 155.3 %collective-permute-start.28 = (bf16[2,8,128,128]{3,2,1,0:T(8,128)(2,1)}, bf16[2,8,128,128]{3,2,1,0:T(8,128)(2,1)}, u32[]{:S(2)}, u32[]{:S(2)}) collective-permute-start(bf16[2,8,128,128]{3,2,1,0:T(8,128)(2,1)} %broadcast_select_fusion.7), channel_id=1, source_target_pairs={{0,32},{2,34},{4,36},{6,38},{8,40},{10,42},{12,44},{14,46},{16,48}... | collective-permute-start | bytes 1572872 | tf_op jit(solution)/shard_map/ppermute | solution.py:15
  (52 other events, 2440.3 us)
Sparse Core Ops, SparseCore 0:
  30.5 343.5 all-reduce.13
  522.2 265.3 all-reduce.9
  1306.7 343.7 all-reduce.11
where the time goes:
time: 1680 us; the launch traced here: 1670 us
  waiting for transfers between devices  829 us (49%)
  blocking collectives  606 us (36%)
  other arithmetic  61.1 us (4%)
  local copies, waits for them, and re-layouts  59.5 us (4%)
  starting transfers between devices  54.6 us (3%)
  matrix products  36.7 us (2%)
  between operations  26.6 us (2%)
    psum x1, blocking collectives, body(): sink_total = lax.psum(sink_part, ('dp', 'ctx'))  329 us
    ppermute x30, waiting for transfers between devices, partner_2(): return lax.ppermute(value, axis, pairs)  311 us
    psum x1, waiting for transfers between devices, broadcast(): return lax.psum(kept, axis)  183 us
    psum x1, waiting for transfers between devices, body(): summed_total, summed_acc = lax.psum((part_total, part_acc), 'ctx')  182 us
    psum x1, waiting for transfers between devices, body(): summed_dq, summed_slots = lax.psum((part_dq, global_slots), 'ctx')  152 us
    psum x1, blocking collectives, body(): summed_dq, summed_slots = lax.psum((part_dq, global_slots), 'ctx')  139 us
    psum x1, blocking collectives, body(): summed_total, summed_acc = lax.psum((part_total, part_acc), 'ctx')  71.4 us
    pmax x1, blocking collectives, body(): global_top = jnp.maximum(lax.pmax(local_top, 'ctx'), sink_logits[:, None])  66.2 us
  transfers between devices with their start and end apart: 37, of which 17 were waited for; matrix products, arithmetic and copies ran while one was open for 7% of the time, Pallas kernels for 0%

commit v1 on v0

--- a/solution.py
+++ b/solution.py
@@ -317,7 +317,8 @@
         ),
     )
     sink_part = -jnp.sum(jnp.exp(sink_logits[:, None] - lse_rows) * row_delta, axis=1)
-    sink_total = lax.psum(sink_part, ("dp", "ctx"))
+    one_axis = lax.psum(sink_part, "ctx")
+    sink_total = lax.psum(one_axis, "dp")
     sink_grad = sink_total / math.sqrt(lax.axis_size("dp") * ctx_count * tokens)
     attention = from_heads(attention_half)[None]
     query_grad = from_heads(query_total.astype(jnp.bfloat16))[None]

time: 1680 us -> 1390 us (0.83)
  blocking collectives: 606 us -> 287 us
    psum x1, blocking collectives: 329 us -> 8.42 us  [body(): sink_total = lax.psum(one_axis, 'dp')]
    psum x1, waiting for transfers between devices: 152 us -> 239 us  [body(): summed_dq, summed_slots = lax.psum((part_dq, global_slots), 'ctx')]
    ppermute x30, waiting for transfers between devices: 311 us -> 240 us  [partner_2(): return lax.ppermute(value, axis, pairs)]
  transfers between devices with their start and end apart: 37 -> 37, of which waited for: 17 -> 18; matrix products, arithmetic and copies ran while one was open for 7% -> 9% of each run, Pallas kernels for 0% -> 0%
where the time goes in v1:
time: 1390 us; the launch traced here: 1380 us
  waiting for transfers between devices  844 us (61%)
  blocking collectives  287 us (21%)
  starting transfers between devices  68.4 us (5%)
  other arithmetic  61.2 us (4%)
  local copies, waits for them, and re-layouts  60.5 us (4%)
  matrix products  36.7 us (3%)
  between operations  26.6 us (2%)
    ppermute x30, waiting for transfers between devices, partner_2(): return lax.ppermute(value, axis, pairs)  240 us
    psum x1, waiting for transfers between devices, body(): summed_dq, summed_slots = lax.psum((part_dq, global_slots), 'ctx')  239 us
    psum x1, waiting for transfers between devices, broadcast(): return lax.psum(kept, axis)  183 us
    psum x1, waiting for transfers between devices, body(): summed_total, summed_acc = lax.psum((part_total, part_acc), 'ctx')  182 us
    psum x1, blocking collectives, body(): summed_dq, summed_slots = lax.psum((part_dq, global_slots), 'ctx')  141 us
    psum x1, blocking collectives, body(): summed_total, summed_acc = lax.psum((part_total, part_acc), 'ctx')  71.4 us
    pmax x1, blocking collectives, body(): global_top = jnp.maximum(lax.pmax(local_top, 'ctx'), sink_logits[:, None])  66.2 us
    ppermute x30, starting transfers between devices, partner_2(): return lax.ppermute(value, axis, pairs)  53 us
  transfers between devices with their start and end apart: 37, of which 18 were waited for; matrix products, arithmetic and copies ran while one was open for 9% of the time, Pallas kernels for 0%

profile of v1, /device:TPU:1, one launch (start us, length us, event | category | flops | bytes accessed | tf_op | source)
XLA Modules:
  0.0 1384.8 jit_solution(13068888172570105390)
XLA Ops:
  66.8 18.5 %collective-permute-done.8 = bf16[128,2048]{1,0:T(8,128)(2,1)} collective-permute-done((bf16[128,2048]{1,0:T(8,128)(2,1)}, bf16[128,2048]{1,0:T(8,128)(2,1)}, u32[]{:S(2)}, u32[]{:S(2)}) %collective-permute-start.8) | collective-permute-done | bytes 524320 | tf_op jit(solution)/shard_map/ppermute | solution.py:15
  90.5 8.0 collective-permute-done.13
  108.9 51.2 %collective-permute-done.9 = bf16[128,2048]{1,0:T(8,128)(2,1)S(1)} collective-permute-done((bf16[128,2048]{1,0:T(8,128)(2,1)S(1)}, bf16[128,2048]{1,0:T(8,128)(2,1)S(1)}, u32[]{:S(2)}, u32[]{:S(2)}) %collective-permute-start.9) | collective-permute-done | bytes 524320 | tf_op jit(solution)/shard_map/ppermute | solution.py:15
  164.5 21.5 %collective-permute-done.14 = bf16[128,2048]{1,0:T(8,128)(2,1)S(1)} collective-permute-done((bf16[128,2048]{1,0:T(8,128)(2,1)S(1)}, bf16[128,2048]{1,0:T(8,128)(2,1)S(1)}, u32[]{:S(2)}, u32[]{:S(2)}) %collective-permute-start.14) | collective-permute-done | bytes 524320 | tf_op jit(solution)/shard_map/ppermute | solution.py:15
  190.6 182.8 %all-reduce.15.cloned.1.call-done = (bf16[4,128,1024]{1,2,0:T(8,128)(2,1)}, bf16[4,128,1024]{1,2,0:T(8,128)(2,1)}) async-done(((bf16[4,128,1024]{1,2,0:T(8,128)(2,1)}, bf16[4,128,1024]{1,2,0:T(8,128)(2,1)}), (bf16[4,128,1024]{1,2,0:T(8,128)(2,1)}, bf16[4,128,1024]{1,2,0:T(8,128)(2,1)})) %all-reduce.15.cloned.1.call-update) | async-done | bytes 2097168 | tf_op jit(solution)/shard_map/psum | solution.py:20
  380.1 66.2 %pmax.7 = f32[8,256]{1,0:T(8,128)S(1)} all-reduce(f32[8,256]{1,0:T(8,128)S(1)} %get-tuple-element.74), channel_id=1, replica_groups=mesh['dp'=4,'ctx'=32,'head'=2] {'ctx'}, use_global_device_ids=true, to_apply=%region_3.4 | all-reduce | flops 2048 | bytes 16384 | tf_op jit(solution)/shard_map/pmax | solution.py:187
  446.6 71.4 %psum.59 = f32[8,256]{1,0:T(8,128)S(1)} all-reduce(f32[8,256]{1,0:T(8,128)S(1)} %fusion.38), channel_id=1, replica_groups=mesh['dp'=4,'ctx'=32,'head'=2] {'ctx'}, use_global_device_ids=true, to_apply=%region_6.7 | all-reduce | flops 2048 | bytes 16384 | tf_op jit(solution)/shard_map/psum | solution.py:196
  528.4 9.0 collective-permute-done.6
  537.5 11.5 collective-permute-done.11
  549.1 11.9 collective-permute-done.16
  572.8 6.5 copy.137
  590.3 6.5 copy.139
  596.7 8.4 fusion.56
  605.1 181.8 %all-reduce.11.cloned.1.call-done = f32[8,256,128]{2,1,0:T(8,128)} async-done(((f32[8,256,128]{2,1,0:T(8,128)}), f32[8,256,128]{2,1,0:T(8,128)}) %all-reduce.11.cloned.1.call-update) | async-done | bytes 1048592 | tf_op jit(solution)/shard_map/psum | solution.py:196
  811.0 141.2 %all-reduce.16 = (bf16[8,256,128]{2,1,0:T(8,128)(2,1)}, f32[8]{0:T(128)S(1)}) all-reduce(f32[8,256,128]{2,1,0:T(8,128)} %convolution_multiply_fusion.2, f32[8]{0:T(128)S(1)} %neg.3), channel_id=1, replica_groups=mesh['dp'=4,'ctx'=32,'head'=2] {'ctx'}, use_global_device_ids=true, to_apply=%region_11.12 | all-reduce | flops 262152 | bytes 1572928 | tf_op jit(solution)/shard_map/psum | solution.py:292
  975.7 8.4 psum.63
  1001.1 29.7 %collective-permute-done.25 = bf16[2,8,128,128]{3,2,1,0:T(8,128)(2,1)S(1)} collective-permute-done((bf16[2,8,128,128]{3,2,1,0:T(8,128)(2,1)}, bf16[2,8,128,128]{3,2,1,0:T(8,128)(2,1)S(1)}, u32[]{:S(2)}, u32[]{:S(2)}) %collective-permute-start.25) | collective-permute-done | bytes 524320 | tf_op jit(solution)/shard_map/ppermute | solution.py:15
  1032.4 14.9 %collective-permute-done.21 = bf16[2,8,128,128]{3,2,1,0:T(8,128)(2,1)S(1)} collective-permute-done((bf16[2,8,128,128]{3,2,1,0:T(8,128)(2,1)S(1)}, bf16[2,8,128,128]{3,2,1,0:T(8,128)(2,1)S(1)}, u32[]{:S(2)}, u32[]{:S(2)}) %collective-permute-start.21) | collective-permute-done | bytes 524320 | tf_op jit(solution)/shard_map/ppermute | solution.py:15
  1047.3 6.8 collective-permute-start.22
  1054.1 11.3 collective-permute-done.31
  1068.9 12.1 collective-permute-done.26
  1081.2 12.1 collective-permute-done.22
  1093.4 21.4 %collective-permute-done.32 = bf16[2,8,128,128]{3,2,1,0:T(8,128)(2,1)S(1)} collective-permute-done((bf16[2,8,128,128]{3,2,1,0:T(8,128)(2,1)S(1)}, bf16[2,8,128,128]{3,2,1,0:T(8,128)(2,1)S(1)}, u32[]{:S(2)}, u32[]{:S(2)}) %collective-permute-start.32) | collective-permute-done | bytes 524320 | tf_op jit(solution)/shard_map/ppermute | solution.py:15
  1122.9 239.2 %all-reduce.13.cloned.1.call-done = f32[2,8,256,128]{3,2,1,0:T(8,128)} async-done(((f32[2,8,256,128]{3,2,1,0:T(8,128)}), f32[2,8,256,128]{3,2,1,0:T(8,128)}) %all-reduce.13.cloned.1.call-update) | async-done | bytes 2097168 | tf_op jit(solution)/shard_map/psum | solution.py:292
  (269 shorter events, 205.7 us)
Async XLA Ops:
  7.2 366.2 %all-reduce.15.cloned.1.call-start = ((), (), s32[]{:S(2)}) async-start(), calls=%async_computation.2 | async-start | bytes 4194304 | tf_op jit(solution)/shard_map/psum | solution.py:20
  15.0 38.0 %collective-permute-start = (bf16[128,2048]{1,0:T(8,128)(2,1)}, bf16[128,2048]{1,0:T(8,128)(2,1)}, u32[]{:S(2)}, u32[]{:S(2)}) collective-permute-start(bf16[128,2048]{1,0:T(8,128)(2,1)} %get-tuple-element.53), channel_id=1, source_target_pairs={{0,2},{2,4},{4,6},{6,8},{8,10},{10,12},{12,14},{14,16},{16,18},{18... | collective-permute-start | bytes 1572872 | tf_op jit(solution)/shard_map/ppermute | solution.py:30
  20.1 33.0 %collective-permute-start.1 = (bf16[128,2048]{1,0:T(8,128)(2,1)}, bf16[128,2048]{1,0:T(8,128)(2,1)}, u32[]{:S(2)}, u32[]{:S(2)}) collective-permute-start(bf16[128,2048]{1,0:T(8,128)(2,1)} %get-tuple-element.54), channel_id=1, source_target_pairs={{2,0},{4,2},{6,4},{8,6},{10,8},{12,10},{14,12},{16,14},{18,16},{20... | collective-permute-start | bytes 1572872 | tf_op jit(solution)/shard_map/ppermute | solution.py:31
  30.4 756.5 %all-reduce.11.cloned.1.call-start = ((), (), s32[]{:S(2)}) async-start(), calls=%async_computation | async-start | bytes 2097152 | tf_op jit(solution)/shard_map/psum | solution.py:196
  49.7 35.6 %collective-permute-start.8 = (bf16[128,2048]{1,0:T(8,128)(2,1)}, bf16[128,2048]{1,0:T(8,128)(2,1)}, u32[]{:S(2)}, u32[]{:S(2)}) collective-permute-start(bf16[128,2048]{1,0:T(8,128)(2,1)} %broadcast_select_fusion.16), channel_id=1, source_target_pairs={{0,4},{2,6},{4,0},{6,2},{8,12},{10,14},{12,8},{14,10},{16,20},{18,... | collective-permute-start | bytes 1572872 | tf_op jit(solution)/shard_map/ppermute | solution.py:15
  51.6 46.9 %collective-permute-start.13 = (bf16[128,2048]{1,0:T(8,128)(2,1)}, bf16[128,2048]{1,0:T(8,128)(2,1)}, u32[]{:S(2)}, u32[]{:S(2)}) collective-permute-start(bf16[128,2048]{1,0:T(8,128)(2,1)} %broadcast_select_fusion.12), channel_id=1, source_target_pairs={{0,4},{2,6},{4,0},{6,2},{8,12},{10,14},{12,8},{14,10},{16,20},{18,... | collective-permute-start | bytes 1572872 | tf_op jit(solution)/shard_map/ppermute | solution.py:15
  62.5 40.4 %collective-permute-start.4 = (bf16[128,2048]{1,0:T(8,128)(2,1)S(1)}, bf16[128,2048]{1,0:T(8,128)(2,1)S(1)}, u32[]{:S(2)}, u32[]{:S(2)}) collective-permute-start(bf16[128,2048]{1,0:T(8,128)(2,1)S(1)} %broadcast_select_fusion.21), channel_id=1, source_target_pairs={{0,8},{2,10},{4,12},{6,14},{8,0},{10,2},{12,4},{14,6},{16,24},{18,... | collective-permute-start | bytes 1572872 | tf_op jit(solution)/shard_map/ppermute | solution.py:15
  86.4 73.7 %collective-permute-start.9 = (bf16[128,2048]{1,0:T(8,128)(2,1)S(1)}, bf16[128,2048]{1,0:T(8,128)(2,1)S(1)}, u32[]{:S(2)}, u32[]{:S(2)}) collective-permute-start(bf16[128,2048]{1,0:T(8,128)(2,1)S(1)} %broadcast_select_fusion.17), channel_id=1, source_target_pairs={{0,8},{2,10},{4,12},{6,14},{8,0},{10,2},{12,4},{14,6},{16,24},{18,... | collective-permute-start | bytes 1572872 | tf_op jit(solution)/shard_map/ppermute | solution.py:15
  99.6 86.4 %collective-permute-start.14 = (bf16[128,2048]{1,0:T(8,128)(2,1)S(1)}, bf16[128,2048]{1,0:T(8,128)(2,1)S(1)}, u32[]{:S(2)}, u32[]{:S(2)}) collective-permute-start(bf16[128,2048]{1,0:T(8,128)(2,1)S(1)} %broadcast_select_fusion.13), channel_id=1, source_target_pairs={{0,8},{2,10},{4,12},{6,14},{8,0},{10,2},{12,4},{14,6},{16,24},{18,... | collective-permute-start | bytes 1572872 | tf_op jit(solution)/shard_map/ppermute | solution.py:15
  103.8 417.7 %collective-permute-start.5 = (bf16[128,2048]{1,0:T(8,128)(2,1)}, bf16[128,2048]{1,0:T(8,128)(2,1)}, u32[]{:S(2)}, u32[]{:S(2)}) collective-permute-start(bf16[128,2048]{1,0:T(8,128)(2,1)} %broadcast_select_fusion.22), channel_id=1, source_target_pairs={{0,16},{2,18},{4,20},{6,22},{8,24},{10,26},{12,28},{14,30},{16,0},... | collective-permute-start | bytes 1572872 | tf_op jit(solution)/shard_map/ppermute | solution.py:15
  160.9 362.1 %collective-permute-start.10 = (bf16[128,2048]{1,0:T(8,128)(2,1)}, bf16[128,2048]{1,0:T(8,128)(2,1)}, u32[]{:S(2)}, u32[]{:S(2)}) collective-permute-start(bf16[128,2048]{1,0:T(8,128)(2,1)} %broadcast_select_fusion.18), channel_id=1, source_target_pairs={{0,16},{2,18},{4,20},{6,22},{8,24},{10,26},{12,28},{14,30},{16,0},... | collective-permute-start | bytes 1572872 | tf_op jit(solution)/shard_map/ppermute | solution.py:15
  186.8 340.1 %collective-permute-start.15 = (bf16[128,2048]{1,0:T(8,128)(2,1)}, bf16[128,2048]{1,0:T(8,128)(2,1)}, u32[]{:S(2)}, u32[]{:S(2)}) collective-permute-start(bf16[128,2048]{1,0:T(8,128)(2,1)} %broadcast_select_fusion.14), channel_id=1, source_target_pairs={{0,16},{2,18},{4,20},{6,22},{8,24},{10,26},{12,28},{14,30},{16,0},... | collective-permute-start | bytes 1572872 | tf_op jit(solution)/shard_map/ppermute | solution.py:15
  521.4 840.8 %all-reduce.13.cloned.1.call-start = ((), (), s32[]{:S(2)}) async-start(), calls=%async_computation.1 | async-start | bytes 4194304 | tf_op jit(solution)/shard_map/psum | solution.py:292
  988.7 382.8 %collective-permute-start.18 = (f32[2,8,128,128]{3,2,1,0:T(8,128)}, f32[2,8,128,128]{3,2,1,0:T(8,128)}, u32[]{:S(2)}, u32[]{:S(2)}) collective-permute-start(f32[2,8,128,128]{3,2,1,0:T(8,128)} %get-tuple-element.37), channel_id=1, source_target_pairs={{0,2},{2,4},{4,6},{6,8},{8,10},{10,12},{12,14},{14,16},{16,18},{18... | collective-permute-start | bytes 3145736 | tf_op jit(solution)/shard_map/ppermute | solution.py:39
  995.0 35.8 %collective-permute-start.25 = (bf16[2,8,128,128]{3,2,1,0:T(8,128)(2,1)}, bf16[2,8,128,128]{3,2,1,0:T(8,128)(2,1)S(1)}, u32[]{:S(2)}, u32[]{:S(2)}) collective-permute-start(bf16[2,8,128,128]{3,2,1,0:T(8,128)(2,1)} %get-tuple-element.45), channel_id=1, source_target_pairs={{0,4},{2,6},{4,0},{6,2},{8,12},{10,14},{12,8},{14,10},{16,20},{18,... | collective-permute-start | bytes 1572872 | tf_op jit(solution)/shard_map/ppermute | solution.py:15
  997.3 50.0 %collective-permute-start.21 = (bf16[2,8,128,128]{3,2,1,0:T(8,128)(2,1)S(1)}, bf16[2,8,128,128]{3,2,1,0:T(8,128)(2,1)S(1)}, u32[]{:S(2)}, u32[]{:S(2)}) collective-permute-start(bf16[2,8,128,128]{3,2,1,0:T(8,128)(2,1)S(1)} %broadcast_select_fusion.9), channel_id=1, source_target_pairs={{0,8},{2,10},{4,12},{6,14},{8,0},{10,2},{12,4},{14,6},{16,24},{18,... | collective-permute-start | bytes 1572872 | tf_op jit(solution)/shard_map/ppermute | solution.py:15
  998.7 66.7 %collective-permute-start.31 = (bf16[2,8,128,128]{3,2,1,0:T(8,128)(2,1)S(1)}, bf16[2,8,128,128]{3,2,1,0:T(8,128)(2,1)S(1)}, u32[]{:S(2)}, u32[]{:S(2)}) collective-permute-start(bf16[2,8,128,128]{3,2,1,0:T(8,128)(2,1)S(1)} %broadcast_select_fusion.1), channel_id=1, source_target_pairs={{0,8},{2,10},{4,12},{6,14},{8,0},{10,2},{12,4},{14,6},{16,24},{18,... | collective-permute-start | bytes 1572872 | tf_op jit(solution)/shard_map/ppermute | solution.py:15
  1031.9 49.1 %collective-permute-start.26 = (bf16[2,8,128,128]{3,2,1,0:T(8,128)(2,1)S(1)}, bf16[2,8,128,128]{3,2,1,0:T(8,128)(2,1)S(1)}, u32[]{:S(2)}, u32[]{:S(2)}) collective-permute-start(bf16[2,8,128,128]{3,2,1,0:T(8,128)(2,1)S(1)} %broadcast_select_fusion.5), channel_id=1, source_target_pairs={{0,8},{2,10},{4,12},{6,14},{8,0},{10,2},{12,4},{14,6},{16,24},{18,... | collective-permute-start | bytes 1572872 | tf_op jit(solution)/shard_map/ppermute | solution.py:15
  1047.3 46.0 %collective-permute-start.22 = (bf16[2,8,128,128]{3,2,1,0:T(8,128)(2,1)S(1)}, bf16[2,8,128,128]{3,2,1,0:T(8,128)(2,1)S(1)}, u32[]{:S(2)}, u32[]{:S(2)}) collective-permute-start(bf16[2,8,128,128]{3,2,1,0:T(8,128)(2,1)S(1)} %broadcast_select_fusion.10), channel_id=1, source_target_pairs={{0,16},{2,18},{4,20},{6,22},{8,24},{10,26},{12,28},{14,30},{16,0},... | collective-permute-start | bytes 1572872 | tf_op jit(solution)/shard_map/ppermute | solution.py:15
  1065.4 49.4 %collective-permute-start.32 = (bf16[2,8,128,128]{3,2,1,0:T(8,128)(2,1)S(1)}, bf16[2,8,128,128]{3,2,1,0:T(8,128)(2,1)S(1)}, u32[]{:S(2)}, u32[]{:S(2)}) collective-permute-start(bf16[2,8,128,128]{3,2,1,0:T(8,128)(2,1)S(1)} %broadcast_select_fusion.2), channel_id=1, source_target_pairs={{0,16},{2,18},{4,20},{6,22},{8,24},{10,26},{12,28},{14,30},{16,0},... | collective-permute-start | bytes 1572872 | tf_op jit(solution)/shard_map/ppermute | solution.py:15
  1081.0 41.0 %collective-permute-start.27 = (bf16[2,8,128,128]{3,2,1,0:T(8,128)(2,1)S(1)}, bf16[2,8,128,128]{3,2,1,0:T(8,128)(2,1)S(1)}, u32[]{:S(2)}, u32[]{:S(2)}) collective-permute-start(bf16[2,8,128,128]{3,2,1,0:T(8,128)(2,1)S(1)} %broadcast_select_fusion.6), channel_id=1, source_target_pairs={{0,16},{2,18},{4,20},{6,22},{8,24},{10,26},{12,28},{14,30},{16,0},... | collective-permute-start | bytes 1572872 | tf_op jit(solution)/shard_map/ppermute | solution.py:15
  1093.3 268.9 %collective-permute-start.23 = (bf16[2,8,128,128]{3,2,1,0:T(8,128)(2,1)S(1)}, bf16[2,8,128,128]{3,2,1,0:T(8,128)(2,1)}, u32[]{:S(2)}, u32[]{:S(2)}) collective-permute-start(bf16[2,8,128,128]{3,2,1,0:T(8,128)(2,1)S(1)} %broadcast_select_fusion.11), channel_id=1, source_target_pairs={{0,32},{2,34},{4,36},{6,38},{8,40},{10,42},{12,44},{14,46},{16,48}... | collective-permute-start | bytes 1572872 | tf_op jit(solution)/shard_map/ppermute | solution.py:15
  1115.7 247.5 %collective-permute-start.33 = (bf16[2,8,128,128]{3,2,1,0:T(8,128)(2,1)}, bf16[2,8,128,128]{3,2,1,0:T(8,128)(2,1)}, u32[]{:S(2)}, u32[]{:S(2)}) collective-permute-start(bf16[2,8,128,128]{3,2,1,0:T(8,128)(2,1)} %broadcast_select_fusion.3), channel_id=1, source_target_pairs={{0,32},{2,34},{4,36},{6,38},{8,40},{10,42},{12,44},{14,46},{16,48}... | collective-permute-start | bytes 1572872 | tf_op jit(solution)/shard_map/ppermute | solution.py:15
  1122.9 242.4 %collective-permute-start.28 = (bf16[2,8,128,128]{3,2,1,0:T(8,128)(2,1)}, bf16[2,8,128,128]{3,2,1,0:T(8,128)(2,1)}, u32[]{:S(2)}, u32[]{:S(2)}) collective-permute-start(bf16[2,8,128,128]{3,2,1,0:T(8,128)(2,1)} %broadcast_select_fusion.7), channel_id=1, source_target_pairs={{0,32},{2,34},{4,36},{6,38},{8,40},{10,42},{12,44},{14,46},{16,48}... | collective-permute-start | bytes 1572872 | tf_op jit(solution)/shard_map/ppermute | solution.py:15
  (53 other events, 2263.1 us)
Sparse Core Ops, SparseCore 0:
  30.5 342.8 all-reduce.14
  521.5 265.3 all-reduce.10
  988.8 373.3 all-reduce.12
